TPU v7x, 256 devices: a whole 4x4x8 slice. The times are simulated.
256 devices in a mesh: ta: 16 (over x_hi, z), ha: 16 (over y, x_lo, core).
Axes of the slice: x: 4 (x_hi: 2, x_lo: 2; x = x_hi * 2 + x_lo), y: 4, z: 8, core: 2. Of those that a mesh axis runs over, the one named last changes fastest.
Arguments:
- queries: bfloat16 [16, 64, 32, 1280], P('ta', 'ha'), may hold values from -6 to 6
- keys: bfloat16 [16, 64, 32, 1280], P('ta', 'ha'), may hold values from -6 to 6
- values: bfloat16 [16, 64, 32, 1280], P('ta', 'ha'), may hold values from -6 to 6
- grad_out: bfloat16 [16, 64, 32, 2560], P('ta', 'ha'), may hold values from -6 to 6
- out_weight: bfloat16 [1280, 2560], P(('ta', 'ha')), may hold values from -0.15625 to 0.15625
- windows: int32 [16, 64, 4, 3], P('ta', 'ha'), may hold values from 0 to 1
Outputs:
- grad_query: bfloat16 [16, 64, 32, 1280], P('ta', 'ha')
- grad_key: bfloat16 [16, 64, 32, 1280], P('ta', 'ha')
- grad_value: bfloat16 [16, 64, 32, 1280], P('ta', 'ha')
- weight_grad: float32 [1280, 2560], P(('ta', 'ha'))
All inputs are finite; a program needn't handle non-finite values.
Results may differ from a plain program's by a relative error of at most 0.024.
Values may be sent and summed in bfloat16 or wider, within the bound.
No kernel may reach another device: no remote copies, remote signals or barrier semaphores. Data moves between devices by JAX's collectives and lax.ppermute only.
A program may use at most 128 MiB of HBM per device.

v0:
```python
import jax
import jax.numpy as jnp
from jax import lax
from jax.sharding import PartitionSpec as P

HEAD_DIM = 64
TILE_W = 8
head_group = 4


def sent_to_all(x, axis):
    peers = lax.axis_size(axis)
    return lax.all_to_all(jnp.broadcast_to(x[None], (peers, *x.shape)), axis, 0, 0, tiled=True)


def joined_along(blocks, dim):
    shape = list(blocks.shape[1:])
    shape[dim] *= blocks.shape[0]
    return jnp.moveaxis(blocks, 0, dim).reshape(shape)


def collect(x, axis, dim):
    blocks = sent_to_all(x, axis)
    return joined_along(blocks, dim)


def padded(block, sides, width):
    for axis, dim in sides:
        count = lax.axis_size(axis)
        forward = [(i, i + 1) for i in range(count - 1)]
        backward = [(target, source) for source, target in forward]
        low = lax.ppermute(
            lax.slice_in_dim(block, block.shape[dim] - width, None, axis=dim), axis, forward
        )
        high = lax.ppermute(lax.slice_in_dim(block, 0, width, axis=dim), axis, backward)
        block = jnp.concatenate([low, block, high], axis=dim)
    return block


def split_up(x, dim, peers):
    before, after = (x.shape[:dim], x.shape[dim + 1 :])
    return jnp.moveaxis(x.reshape(*before, peers, -1, *after), dim, 0)


def sent_and_summed(x, axis, dim):
    peers = lax.axis_size(axis)
    blocks = lax.all_to_all(split_up(x, dim, peers), axis, 0, 0, tiled=True)
    return jnp.sum(blocks, axis=0)


def shifted(value, axis, steps):
    count = lax.axis_size(axis)
    first, last = (max(0, -steps), min(count, count - steps))
    return lax.ppermute(value, axis, [(source, source + steps) for source in range(first, last)])


def grid_positions(first_time, first_row, frames, row_count, col_count):
    grid_shape = (frames, row_count, col_count)
    time_index = first_time + lax.broadcasted_iota(jnp.int32, grid_shape, 0)
    row_index = first_row + lax.broadcasted_iota(jnp.int32, grid_shape, 1)
    tile_index = lax.broadcasted_iota(jnp.int32, grid_shape, 2) // TILE_W
    return jnp.stack([time_index, row_index, tile_index], axis=-1).reshape(-1, 3)


def visible(query_pos, query_ext, query_valid, key_pos, key_valid):
    distance = jnp.abs(query_pos[:, None, :] - key_pos[None, :, :])
    inside = jnp.all(distance <= query_ext[:, None, :], axis=2)
    return inside & query_valid[:, None] & key_valid[None, :]


def split_heads(tensor):
    return tensor.reshape(tensor.shape[0], -1, head_group, HEAD_DIM).transpose(1, 2, 0, 3)


def split_stats(tensor):
    return tensor.reshape(tensor.shape[0], -1, head_group).transpose(1, 2, 0)


def merge_heads(tensor):
    return tensor.transpose(2, 0, 1, 3).reshape(tensor.shape[2], -1)


def merge_stats(tensor):
    return tensor.transpose(2, 0, 1).reshape(tensor.shape[2], -1)


def masked_scores(query_group, key_group, allowed):
    raw_scores = jnp.einsum(
        "hqd,hkd->hqk", query_group, key_group, preferred_element_type=jnp.float32
    ) * HEAD_DIM ** (-0.5)
    return jnp.where(allowed[None], raw_scores, -1e30)


def attend(flat_queries, flat_keys, flat_values, allowed):

    def attend_one_group(inputs):
        query_group, key_group, value_group = inputs
        scores = masked_scores(query_group, key_group, allowed)
        row_max = jnp.max(scores, axis=2, keepdims=True)
        row_total = jnp.sum(
            jnp.where(allowed[None], jnp.exp(scores - row_max), 0.0), axis=2, keepdims=True
        )
        log_total = row_max + jnp.log(row_total)
        attention = jnp.where(allowed[None], jnp.exp(scores - log_total), 0.0).astype(jnp.bfloat16)
        combined = jnp.einsum(
            "hqk,hkd->hqd", attention, value_group, preferred_element_type=jnp.float32
        )
        return (combined.astype(jnp.bfloat16), log_total[..., 0])

    combined, log_total = lax.map(
        attend_one_group,
        (split_heads(flat_queries), split_heads(flat_keys), split_heads(flat_values)),
    )
    return (merge_heads(combined), merge_stats(log_total))


def attention_grads(
    flat_queries, flat_grads, log_total, row_delta, flat_keys, flat_values, allowed
):

    def attention_one_group(inputs):
        query_group, grad_group, total_group, delta_group, key_group, value_group = inputs
        scores = masked_scores(query_group, key_group, allowed)
        recomputed = jnp.where(allowed[None], jnp.exp(scores - total_group[:, :, None]), 0.0)
        value_grad = jnp.einsum(
            "hqk,hqd->hkd",
            recomputed.astype(jnp.bfloat16),
            grad_group,
            preferred_element_type=jnp.float32,
        )
        score_grad = jnp.einsum(
            "hqd,hkd->hqk", grad_group, value_group, preferred_element_type=jnp.float32
        )
        rounded_grad = (recomputed * (score_grad - delta_group[:, :, None])).astype(jnp.bfloat16)
        query_grad = jnp.einsum(
            "hqk,hkd->hqd", rounded_grad, key_group, preferred_element_type=jnp.float32
        ) * HEAD_DIM ** (-0.5)
        key_grad = jnp.einsum(
            "hqk,hqd->hkd", rounded_grad, query_group, preferred_element_type=jnp.float32
        ) * HEAD_DIM ** (-0.5)
        return (query_grad, key_grad, value_grad)

    head_grads = lax.map(
        attention_one_group,
        (
            split_heads(flat_queries),
            split_heads(flat_grads),
            split_stats(log_total),
            split_stats(row_delta),
            split_heads(flat_keys),
            split_heads(flat_values),
        ),
    )
    return (merge_heads(head_grads[0]), merge_heads(head_grads[1]), merge_heads(head_grads[2]))


def inside_grid(positions, all_frames, all_rows):
    return (
        (positions[:, 0] >= 0)
        & (positions[:, 0] < all_frames)
        & (positions[:, 1] >= 0)
        & (positions[:, 1] < all_rows)
    )


def local(queries, keys, values, grad_out, out_weight, windows):
    frames, row_count, col_count, inner = queries.shape
    model_width = grad_out.shape[3]
    token_count = frames * row_count * col_count
    time_index = lax.axis_index("ta")
    row_index = lax.axis_index("ha")
    all_frames = frames * lax.axis_size("ta")
    all_rows = row_count * lax.axis_size("ha")
    total_tokens = all_frames * all_rows * col_count
    weight = lax.all_gather(collect(out_weight, "ha", 0), "ta", axis=0, tiled=True)
    flat_grad = grad_out.reshape(token_count, model_width)
    grad_attn = lax.dot_general(
        flat_grad, weight, (((1,), (1,)), ((), ())), preferred_element_type=jnp.float32
    ).astype(jnp.bfloat16)
    joined = jnp.concatenate([keys, values], axis=3)
    nearby = padded(joined, (("ta", 0), ("ha", 1)), 1)
    near_keys = nearby[..., :inner].reshape(-1, inner)
    near_values = nearby[..., inner:].reshape(-1, inner)
    own_pos = grid_positions(time_index, row_index * row_count, frames, row_count, col_count)
    near_pos = grid_positions(
        time_index - 1, row_index * row_count - 1, frames + 2, row_count + 2, col_count
    )
    near_valid = inside_grid(near_pos, all_frames, all_rows)
    own_valid = jnp.ones((token_count,), jnp.bool_)
    own_ext = jnp.repeat(windows, TILE_W, axis=2).reshape(-1, 3)
    allowed = visible(own_pos, own_ext, own_valid, near_pos, near_valid)
    flat_queries = queries.reshape(token_count, inner)
    attended, log_total = attend(flat_queries, near_keys, near_values, allowed)
    row_delta = jnp.sum(
        (grad_attn.astype(jnp.float32) * attended.astype(jnp.float32)).reshape(
            token_count, -1, HEAD_DIM
        ),
        axis=2,
    )
    factor = total_tokens ** (-0.5)
    frame_rows = lax.psum_scatter(
        lax.dot_general(
            attended, flat_grad, (((0,), (0,)), ((), ())), preferred_element_type=jnp.float32
        )
        * factor,
        "ta",
        scatter_dimension=0,
        tiled=True,
    )
    weight_grad = sent_and_summed(frame_rows, "ha", 0)
    query_grad, near_key_grad, near_value_grad = attention_grads(
        flat_queries, grad_attn, log_total, row_delta, near_keys, near_values, allowed
    )
    joined_grads = jnp.concatenate([near_key_grad, near_value_grad], axis=1).reshape(
        frames + 2, row_count + 2, col_count, 2 * inner
    )
    centre = joined_grads[1]
    for offset, piece in ((-1, joined_grads[0]), (1, joined_grads[2])):
        centre = centre + shifted(piece, "ta", offset)
    middle = centre[1 : row_count + 1]
    for offset, piece, target in ((1, centre[row_count + 1], 0), (-1, centre[0], row_count - 1)):
        middle = middle.at[target].add(shifted(piece, "ha", offset))
    key_grad = middle[..., :inner]
    value_grad = middle[..., inner:]
    return (
        query_grad.astype(jnp.bfloat16).reshape(queries.shape),
        key_grad.astype(jnp.bfloat16).reshape(queries.shape),
        value_grad.astype(jnp.bfloat16).reshape(queries.shape),
        weight_grad,
    )


def solution(mesh):
    placed = (
        P("ta", "ha", None, None),
        P("ta", "ha", None, None),
        P("ta", "ha", None, None),
        P("ta", "ha", None, None),
        P(("ta", "ha"), None),
        P("ta", "ha", None, None),
    )
    return jax.shard_map(
        local,
        mesh=mesh,
        in_specs=placed,
        out_specs=(
            P("ta", "ha", None, None),
            P("ta", "ha", None, None),
            P("ta", "ha", None, None),
            P(("ta", "ha"), None),
        ),
        check_vma=False,
    )
```

profile of v0, /device:TPU:1, one launch (start us, length us, event | category | flops | bytes accessed | tf_op | source)
XLA Modules:
  0.0 488.2 jit_solution(15356258504741467919)
XLA Ops:
  8.2 18.4 %all_to_all.10 = bf16[16,5,2560]{2,1,0:T(8,128)(2,1)S(1)} all-to-all(bf16[16,5,2560]{2,1,0:T(8,128)(2,1)S(1)} %broadcast_in_dim.88), channel_id=1, replica_groups=mesh['ta'=16,'ha'=16] {'ha'}, dimensions={0} | all-to-all | bytes 819200 | tf_op jit(solution)/shard_map/all_to_all | solution.py:13
  27.7 1.4 collective-permute-start.1
  29.1 4.2 collective-permute-start
  33.8 13.7 %collective-permute-done.1 = bf16[1,4,32,2560]{3,2,1,0:T(8,128)(2,1)S(1)} collective-permute-done((bf16[1,4,32,2560]{3,2,1,0:T(8,128)(2,1)S(1)}, bf16[1,4,32,2560]{3,2,1,0:T(8,128)(2,1)S(1)}, u32[]{:S(2)}, u32[]{:S(2)}) %collective-permute-start.1) | collective-permute-done | bytes 655392 | tf_op jit(solution)/shard_map/ppermute | solution.py:35
  47.6 2.4 collective-permute-done
  51.2 4.9 collective-permute-start.2
  56.1 1.9 collective-permute-start.3
  60.5 5.0 %collective-permute-done.2 = bf16[3,1,32,2560]{3,2,1,0:T(8,128)(2,1)} collective-permute-done((bf16[3,1,32,2560]{3,2,1,0:T(8,128)(2,1)}, bf16[3,1,32,2560]{3,2,1,0:T(8,128)(2,1)}, u32[]{:S(2)}, u32[]{:S(2)}) %collective-permute-start.2) | collective-permute-done | bytes 491552 | tf_op jit(solution)/shard_map/ppermute | solution.py:32
  65.5 7.1 %collective-permute-done.3 = bf16[3,1,32,2560]{3,2,1,0:T(8,128)(2,1)} collective-permute-done((bf16[3,1,32,2560]{3,2,1,0:T(8,128)(2,1)}, bf16[3,1,32,2560]{3,2,1,0:T(8,128)(2,1)}, u32[]{:S(2)}, u32[]{:S(2)}) %collective-permute-start.3) | collective-permute-done | bytes 491552 | tf_op jit(solution)/shard_map/ppermute | solution.py:35
  72.6 1.7 pad_maximum_fusion
  74.3 1.5 fusion.54
  75.8 4.7 reshape_reshape.14
  80.4 5.1 %copy.37 = bf16[5,4,576,64]{2,3,1,0:T(8,128)(2,1)} copy(bf16[5,4,576,64]{3,1,0,2:T(4,128)(2,1)} %bitcast.149) | data formatting | bytes 2949120 | tf_op jit(solution)/shard_map/while | solution.py:110
  85.5 3.0 reshape_reshape.13
  88.5 4.3 copy.42
  92.8 10.1 %while.28 = (s32[]{:T(128)}, bf16[5,4,128,64]{2,3,1,0:T(8,128)(2,1)S(1)}, f32[5,4,128]{2,1,0:T(4,128)S(1)}, pred[128,576]{0,1:T(8,128)(4,1)S(1)}, bf16[5,4,128,6...) while((s32[]{:T(128)}, ...), condition=%wide.region_4.5_spmd, body=%wide.region_1.4_spmd.sunk | while | flops 78183936 | bytes 4565089 | solution.py:110
  102.9 6.6 %convolution_multiply_fusion.4 = f32[1280,2560]{1,0:T(8,128)} fusion(bf16[128,1280]{0,1:T(8,128)(2,1)S(1)} %bitcast.159, bf16[128,2560]{1,0:T(8,128)(2,1)S(1)} %bitcast.148), kind=kOutput, calls=%fused_computation.61 | convolution fusion | flops 842137600 | bytes 14090240 | tf_op jit(solution)/shard_map/dot_general | solution.py:202
  110.4 45.5 %all-gather.2.cloned.1.call-done = bf16[1280,2560]{1,0:T(8,128)(2,1)} async-done(((bf16[80,2560]{1,0:T(8,128)(2,1)}), bf16[1280,2560]{1,0:T(8,128)(2,1)}) %all-gather.2.cloned.1.call-update) | async-done | bytes 6553616 | tf_op jit(solution)/shard_map/all_gather | solution.py:175
  155.9 5.8 %convert_multiply_fusion = (f32[128,1280]{1,0:T(8,128)S(1)}, bf16[128,1280]{1,0:T(8,128)(2,1)}) fusion(bf16[128,1280]{1,0:T(8,128)(2,1)} %copy.39, bf16[128,2560]{1,0:T(8,128)(2,1)S(1)} %bitcast.147, bf16[1280,2560]{1,0:T(8,128)(2,1)} %all-gather.2.cloned.1.call-done), kind=kOutput, calls=%fused_computation.74 | convolution fusion | flops 839516160 | bytes 8519680 | tf_op jit(solution)/shard_map/dot_general | solution.py:177
  163.1 25.7 %while.29 = (s32[]{:T(128)}, bf16[5,4,128,64]{2,3,1,0:T(8,128)(2,1)}, f32[5,4,576,64]{2,3,1,0:T(8,128)}, f32[5,4,576,64]{2,3,1,0:T(8,128)}, pred[128,576]{0,1:T(...) while((s32[]{:T(128)}, ...), condition=%wide.region_7.8_spmd, body=%wide.region_6.7_spmd.sunk | while | flops 191283200 | bytes 8086657 | solution.py:143
  188.8 2.4 copy.46
  191.3 3.6 copy.45
  194.9 2.7 fusion.48
  198.9 4.1 collective-permute-start.5
  203.0 77.8 %collective-permute-done.4 = f32[6,32,2560]{2,1,0:T(8,128)S(1)} collective-permute-done((f32[6,32,2560]{2,1,0:T(8,128)S(1)}, f32[6,32,2560]{2,1,0:T(8,128)S(1)}, u32[]{:S(2)}, u32[]{:S(2)}) %collective-permute-start.4) | collective-permute-done | bytes 1966112 | tf_op jit(solution)/shard_map/ppermute | solution.py:54
  282.2 3.2 collective-permute-start.6
  287.6 1.9 collective-permute-start.7
  289.5 4.8 collective-permute-done.6
  295.3 156.6 %reduce-scatter.2.cloned.1.call-done = f32[80,2560]{1,0:T(8,128)} async-done(((f32[1280,2560]{1,0:T(8,128)}), f32[80,2560]{1,0:T(8,128)}) %reduce-scatter.2.cloned.1.call-update) | async-done | bytes 819216 | tf_op jit(solution)/shard_map/reduce_scatter | solution.py:201
  451.9 2.4 reshape.352
  454.3 7.8 %all-to-all-start.1 = ((f32[16,5,2560]{2,1,0:T(8,128)}), f32[16,5,2560]{2,1,0:T(8,128)S(1)}, u32[]{:S(2)}, u32[]{:S(2)}) async-start(f32[16,5,2560]{2,1,0:T(8,128)} %reshape.352), calls=%async_computation.2 | async-start | bytes 2621440 | tf_op jit(solution)/shard_map/all_to_all | solution.py:47
  464.2 16.4 %all-to-all-done.1 = f32[16,5,2560]{2,1,0:T(8,128)S(1)} async-done(((f32[16,5,2560]{2,1,0:T(8,128)}), f32[16,5,2560]{2,1,0:T(8,128)S(1)}, u32[]{:S(2)}, u32[]{:S(2)}) %all-to-all-start.1) | async-done | bytes 819232 | tf_op jit(solution)/shard_map/all_to_all | solution.py:47
  (128 shorter events, 52.6 us)
Async XLA Ops:
  7.2 95.7 %copy-start = (bf16[1,4,32,2560]{3,2,1,0:T(8,128)(2,1)S(1)}, bf16[1,4,32,2560]{3,2,1,0:T(8,128)(2,1)}, u32[]{:S(2)}) copy-start(bf16[1,4,32,2560]{3,2,1,0:T(8,128)(2,1)} %param.17) | copy-start | bytes 1966084
  7.2 20.4 %copy-start.4 = (bf16[1,4,32,1280]{3,2,1,0:T(8,128)(2,1)S(1)}, bf16[1,4,32,1280]{3,2,1,0:T(8,128)(2,1)}, u32[]{:S(2)}) copy-start(bf16[1,4,32,1280]{3,2,1,0:T(8,128)(2,1)} %param.15) | copy-start | bytes 983044
  7.2 20.4 %copy-start.5 = (bf16[1,4,32,1280]{3,2,1,0:T(8,128)(2,1)S(1)}, bf16[1,4,32,1280]{3,2,1,0:T(8,128)(2,1)}, u32[]{:S(2)}) copy-start(bf16[1,4,32,1280]{3,2,1,0:T(8,128)(2,1)} %param.16) | copy-start | bytes 983044
  7.2 148.7 %all-gather.2.cloned.1.call-start = ((), (), s32[]{:S(2)}) async-start(), calls=%async_computation.3 | async-start | bytes 6963200 | tf_op jit(solution)/shard_map/all_gather | solution.py:175
  27.5 424.4 %reduce-scatter.2.cloned.1.call-start = ((), (), s32[]{:S(2)}) async-start(), calls=%async_computation.4 | async-start | bytes 13926400 | tf_op jit(solution)/shard_map/reduce_scatter | solution.py:201
  27.6 30.8 %copy-start.8 = (s32[1,4,4,3]{2,1,3,0:T(4,128)S(1)}, s32[1,4,4,3]{2,1,3,0:T(4,128)}, u32[]{:S(2)}) copy-start(s32[1,4,4,3]{2,1,3,0:T(4,128)} %param.19) | copy-start | bytes 580
  27.7 31.0 %copy-start.6 = (bf16[1,4,32,1280]{3,2,1,0:T(8,128)(2,1)S(1)}, bf16[1,4,32,1280]{3,2,1,0:T(8,128)(2,1)}, u32[]{:S(2)}) copy-start(bf16[1,4,32,1280]{3,2,1,0:T(8,128)(2,1)} %param.14) | copy-start | bytes 983044
  27.7 19.9 %collective-permute-start.1 = (bf16[1,4,32,2560]{3,2,1,0:T(8,128)(2,1)S(1)}, bf16[1,4,32,2560]{3,2,1,0:T(8,128)(2,1)S(1)}, u32[]{:S(2)}, u32[]{:S(2)}) collective-permute-start(bf16[1,4,32,2560]{3,2,1,0:T(8,128)(2,1)S(1)} %constant_dynamic-update-slice_fusion), channel_id=1, source_target_pairs={{16,0},{32,16},{48,32},{64,48},{80,64},{96,80},{112,96},{128,112},... | collective-permute-start | bytes 1966088 | tf_op jit(solution)/shard_map/ppermute | solution.py:35
  29.1 20.9 %collective-permute-start = (bf16[1,4,32,2560]{3,2,1,0:T(8,128)(2,1)S(1)}, bf16[1,4,32,2560]{3,2,1,0:T(8,128)(2,1)S(1)}, u32[]{:S(2)}, u32[]{:S(2)}) collective-permute-start(bf16[1,4,32,2560]{3,2,1,0:T(8,128)(2,1)S(1)} %constant_dynamic-update-slice_fusion), channel_id=1, source_target_pairs={{0,16},{16,32},{32,48},{48,64},{64,80},{80,96},{96,112},{112,128},... | collective-permute-start | bytes 1966088 | tf_op jit(solution)/shard_map/ppermute | solution.py:32
  50.0 8.6 %copy-start.2 = (bf16[1,4,32,2560]{3,2,1,0:T(8,128)(2,1)}, bf16[1,4,32,2560]{3,2,1,0:T(8,128)(2,1)S(1)}, u32[]{:S(2)}) copy-start(bf16[1,4,32,2560]{3,2,1,0:T(8,128)(2,1)S(1)} %collective-permute-done) | copy-start | bytes 1966084
  51.2 14.3 %collective-permute-start.2 = (bf16[3,1,32,2560]{3,2,1,0:T(8,128)(2,1)}, bf16[3,1,32,2560]{3,2,1,0:T(8,128)(2,1)}, u32[]{:S(2)}, u32[]{:S(2)}) collective-permute-start(bf16[3,1,32,2560]{3,2,1,0:T(8,128)(2,1)} %get-tuple-element.215), channel_id=1, source_target_pairs={{0,1},{1,2},{2,3},{3,4},{4,5},{5,6},{6,7},{7,8},{8,9},{9,10},{10,1... | collective-permute-start | bytes 1474568 | tf_op jit(solution)/shard_map/ppermute | solution.py:32
  56.1 16.5 %collective-permute-start.3 = (bf16[3,1,32,2560]{3,2,1,0:T(8,128)(2,1)}, bf16[3,1,32,2560]{3,2,1,0:T(8,128)(2,1)}, u32[]{:S(2)}, u32[]{:S(2)}) collective-permute-start(bf16[3,1,32,2560]{3,2,1,0:T(8,128)(2,1)} %get-tuple-element.216), channel_id=1, source_target_pairs={{1,0},{2,1},{3,2},{4,3},{5,4},{6,5},{7,6},{8,7},{9,8},{10,9},{11,1... | collective-permute-start | bytes 1474568 | tf_op jit(solution)/shard_map/ppermute | solution.py:35
  88.5 4.3 copy-start.3
  197.6 83.2 %collective-permute-start.4 = (f32[6,32,2560]{2,1,0:T(8,128)S(1)}, f32[6,32,2560]{2,1,0:T(8,128)S(1)}, u32[]{:S(2)}, u32[]{:S(2)}) collective-permute-start(f32[6,32,2560]{2,1,0:T(8,128)S(1)} %bitcast.158), channel_id=1, source_target_pairs={{16,0},{32,16},{48,32},{64,48},{80,64},{96,80},{112,96},{128,112},... | collective-permute-start | bytes 5898248 | tf_op jit(solution)/shard_map/ppermute | solution.py:54
  198.9 81.9 %collective-permute-start.5 = (f32[6,32,2560]{2,1,0:T(8,128)S(1)}, f32[6,32,2560]{2,1,0:T(8,128)S(1)}, u32[]{:S(2)}, u32[]{:S(2)}) collective-permute-start(f32[6,32,2560]{2,1,0:T(8,128)S(1)} %bitcast.157), channel_id=1, source_target_pairs={{0,16},{16,32},{32,48},{48,64},{64,80},{80,96},{96,112},{112,128},... | collective-permute-start | bytes 5898248 | tf_op jit(solution)/shard_map/ppermute | solution.py:54
  280.9 4.5 copy-start.7
  282.2 12.1 %collective-permute-start.6 = (f32[32,2560]{1,0:T(8,128)}, f32[32,2560]{1,0:T(8,128)}, u32[]{:S(2)}, u32[]{:S(2)}) collective-permute-start(f32[32,2560]{1,0:T(8,128)} %get-tuple-element.214), channel_id=1, source_target_pairs={{0,1},{1,2},{2,3},{3,4},{4,5},{5,6},{6,7},{7,8},{8,9},{9,10},{10,1... | collective-permute-start | bytes 983048 | tf_op jit(solution)/shard_map/ppermute | solution.py:54
  287.6 174.5 %collective-permute-start.7 = (f32[32,2560]{1,0:T(8,128)}, f32[32,2560]{1,0:T(8,128)}, u32[]{:S(2)}, u32[]{:S(2)}) collective-permute-start(f32[32,2560]{1,0:T(8,128)} %get-tuple-element.213), channel_id=1, source_target_pairs={{1,0},{2,1},{3,2},{4,3},{5,4},{6,5},{7,6},{8,7},{9,8},{10,9},{11,1... | collective-permute-start | bytes 983048 | tf_op jit(solution)/shard_map/ppermute | solution.py:54
  454.3 26.3 %all-to-all-start.1 = ((f32[16,5,2560]{2,1,0:T(8,128)}), f32[16,5,2560]{2,1,0:T(8,128)S(1)}, u32[]{:S(2)}, u32[]{:S(2)}) async-start(f32[16,5,2560]{2,1,0:T(8,128)} %reshape.352), calls=%async_computation.2 | async-start | bytes 2621440 | tf_op jit(solution)/shard_map/all_to_all | solution.py:47
  462.1 19.2 %copy-start.1 = (bf16[1,4,32,2560]{3,2,1,0:T(8,128)(2,1)S(1)}, bf16[1,4,32,2560]{3,2,1,0:T(8,128)(2,1)}, u32[]{:S(2)}) copy-start(bf16[1,4,32,2560]{3,2,1,0:T(8,128)(2,1)} %param.17) | copy-start | bytes 1966084
Sparse Core Ops, SparseCore 0:
  27.7 128.1 all-gather.1
  160.1 291.8 reduce-scatter.1
where the time goes:
time: 489 us; the launch traced here: 488 us
  waiting for transfers between devices  329 us (67%)
  matrix products  46.6 us (10%)
  local copies, waits for them, and re-layouts  37.3 us (8%)
  starting transfers between devices  30.8 us (6%)
  blocking collectives  18.4 us (4%)
  between operations  14.5 us (3%)
  other arithmetic  10.9 us (2%)
    reduce_scatter x1, waiting for transfers between devices, local(): lax.psum_scatter(lax.dot_general(attended, flat_grad, (((0,), (0,)), ((),...  157 us
    ppermute x4, waiting for transfers between devices, shifted(): lax.ppermute(value, axis, [(source, source + steps) for source in range(f...  82.6 us
    all_gather x1, waiting for transfers between devices, local(): lax.all_gather(collect(out_weight, 'ha', 0), 'ta', axis=0, tiled=True)  45.5 us
    ppermute x2, waiting for transfers between devices, padded(): lax.ppermute(lax.slice_in_dim(block, 0, width, axis=dim), axis, backward)  20.9 us
    all_to_all x1, blocking collectives, sent_to_all(): lax.all_to_all(jnp.broadcast_to(x[None], (peers, *x.shape)), axis, 0, 0,...  18.4 us
    all_to_all x1, waiting for transfers between devices, sent_and_summed(): blocks = lax.all_to_all(split_up(x, dim, peers), axis, 0, 0, tiled=True)  16.4 us
    ppermute x4, starting transfers between devices, shifted(): lax.ppermute(value, axis, [(source, source + steps) for source in range(f...  10.5 us
  transfers between devices with their start and end apart: 11, of which 9 were waited for; matrix products, arithmetic and copies ran while one was open for 19% of the time, Pallas kernels for 0%

commit v1 on v0

--- a/solution.py
+++ b/solution.py
@@ -172,7 +172,10 @@
     all_frames = frames * lax.axis_size("ta")
     all_rows = row_count * lax.axis_size("ha")
     total_tokens = all_frames * all_rows * col_count
-    weight = lax.all_gather(collect(out_weight, "ha", 0), "ta", axis=0, tiled=True)
+    weight = jnp.concatenate(
+        lax.all_to_all(jnp.stack([collect(out_weight, "ha", 0)] * lax.axis_size("ta")), "ta", 0, 0),
+        axis=0,
+    )
     flat_grad = grad_out.reshape(token_count, model_width)
     grad_attn = lax.dot_general(
         flat_grad, weight, (((1,), (1,)), ((), ())), preferred_element_type=jnp.float32

time: 489 us -> 571 us (1.17)
  waiting for transfers between devices: 329 us -> 386 us
  starting transfers between devices: 30.8 us -> 46.5 us
  local copies, waits for them, and re-layouts: 37.3 us -> 44.3 us
    all_to_all x0 -> x1, waiting for transfers between devices: none -> 192 us  [local(): lax.all_to_all(jnp.stack([collect(out_weight, 'ha', 0)] * lax.axis_size('...]
    reduce_scatter x1, waiting for transfers between devices: 157 us -> 109 us  [local(): lax.psum_scatter(lax.dot_general(attended, flat_grad, (((0,), (0,)), ((),...]
    all_gather x1 -> x0, waiting for transfers between devices: 45.5 us -> none  [local(): lax.all_gather(collect(out_weight, 'ha', 0), 'ta', axis=0, tiled=True)]
    ppermute x4, waiting for transfers between devices: 82.6 us -> 46.2 us  [shifted(): lax.ppermute(value, axis, [(source, source + steps) for source in range(f...]
    all_to_all x0 -> x1, starting transfers between devices: none -> 13.4 us  [local(): lax.all_to_all(jnp.stack([collect(out_weight, 'ha', 0)] * lax.axis_size('...]
    ppermute x2, waiting for transfers between devices: 20.9 us -> 11.1 us  [padded(): lax.ppermute(lax.slice_in_dim(block, 0, width, axis=dim), axis, backward)]
    ppermute x2, waiting for transfers between devices: 7.42 us -> 13.2 us  [padded(): lax.ppermute(lax.slice_in_dim(block, block.shape[dim] - width, None, axis...]
  transfers between devices with their start and end apart: 11 -> 11, of which waited for: 9 -> 10; matrix products, arithmetic and copies ran while one was open for 19% -> 11% of each run, Pallas kernels for 0% -> 0%
where the time goes in v1:
time: 571 us; the launch traced here: 570 us
  waiting for transfers between devices  386 us (68%)
  matrix products  46.8 us (8%)
  starting transfers between devices  46.5 us (8%)
  local copies, waits for them, and re-layouts  44.3 us (8%)
  blocking collectives  16.9 us (3%)
  other arithmetic  14.5 us (3%)
  between operations  14.4 us (3%)
    all_to_all x1, waiting for transfers between devices, local(): lax.all_to_all(jnp.stack([collect(out_weight, 'ha', 0)] * lax.axis_size('...  192 us
    reduce_scatter x1, waiting for transfers between devices, local(): lax.psum_scatter(lax.dot_general(attended, flat_grad, (((0,), (0,)), ((),...  109 us
    ppermute x4, waiting for transfers between devices, shifted(): lax.ppermute(value, axis, [(source, source + steps) for source in range(f...  46.2 us
    all_to_all x1, blocking collectives, sent_to_all(): lax.all_to_all(jnp.broadcast_to(x[None], (peers, *x.shape)), axis, 0, 0,...  16.9 us
    all_to_all x1, waiting for transfers between devices, sent_and_summed(): blocks = lax.all_to_all(split_up(x, dim, peers), axis, 0, 0, tiled=True)  14.3 us
    all_to_all x1, starting transfers between devices, local(): lax.all_to_all(jnp.stack([collect(out_weight, 'ha', 0)] * lax.axis_size('...  13.4 us
    ppermute x2, waiting for transfers between devices, padded(): lax.ppermute(lax.slice_in_dim(block, block.shape[dim] - width, None, axis...  13.2 us
    ppermute x4, starting transfers between devices, shifted(): lax.ppermute(value, axis, [(source, source + steps) for source in range(f...  13 us
  transfers between devices with their start and end apart: 11, of which 10 were waited for; matrix products, arithmetic and copies ran while one was open for 11% of the time, Pallas kernels for 0%

profile of v1, /device:TPU:1, one launch (start us, length us, event | category | flops | bytes accessed | tf_op | source)
XLA Modules:
  0.0 569.6 jit_solution(18278222983059897662)
XLA Ops:
  9.4 4.4 collective-permute-start
  15.6 11.6 %collective-permute-done = bf16[1,4,32,2560]{3,2,1,0:T(8,128)(2,1)S(1)} collective-permute-done((bf16[1,4,32,2560]{3,2,1,0:T(8,128)(2,1)S(1)}, bf16[1,4,32,2560]{3,2,1,0:T(8,128)(2,1)S(1)}, u32[]{:S(2)}, u32[]{:S(2)}) %collective-permute-start) | collective-permute-done | bytes 655392 | tf_op jit(solution)/shard_map/ppermute | solution.py:32
  27.1 4.2 collective-permute-done.1
  32.4 4.7 collective-permute-start.2
  37.1 1.9 collective-permute-start.3
  43.2 7.0 %collective-permute-done.3 = bf16[3,1,32,2560]{3,2,1,0:T(8,128)(2,1)} collective-permute-done((bf16[3,1,32,2560]{3,2,1,0:T(8,128)(2,1)}, bf16[3,1,32,2560]{3,2,1,0:T(8,128)(2,1)}, u32[]{:S(2)}, u32[]{:S(2)}) %collective-permute-start.3) | collective-permute-done | bytes 491552 | tf_op jit(solution)/shard_map/ppermute | solution.py:35
  50.2 1.9 pad_maximum_fusion
  53.5 4.7 reshape_reshape.14
  58.2 5.1 copy.37
  63.3 3.0 reshape_reshape.13
  66.3 4.2 copy.42
  70.5 10.1 %while.28 = (s32[]{:T(128)}, bf16[5,4,128,64]{2,3,1,0:T(8,128)(2,1)S(1)}, f32[5,4,128]{2,1,0:T(4,128)S(1)}, pred[128,576]{0,1:T(8,128)(4,1)S(1)}, bf16[5,4,128,6...) while((s32[]{:T(128)}, ...), condition=%wide.region_4.5_spmd, body=%wide.region_1.4_spmd.sunk | while | flops 78183936 | bytes 4565081 | solution.py:110
  80.6 6.6 %convolution_multiply_fusion.4 = f32[1280,2560]{1,0:T(8,128)} fusion(bf16[128,1280]{0,1:T(8,128)(2,1)S(1)} %bitcast.160, bf16[128,2560]{1,0:T(8,128)(2,1)S(1)} %bitcast.149), kind=kOutput, calls=%fused_computation.61 | convolution fusion | flops 842137600 | bytes 14090240 | tf_op jit(solution)/shard_map/dot_general | solution.py:205
  88.0 16.9 %all_to_all.15 = bf16[16,5,2560]{2,1,0:T(8,128)(2,1)} all-to-all(bf16[16,5,2560]{2,1,0:T(8,128)(2,1)S(1)} %broadcast_in_dim.88), channel_id=1, replica_groups=mesh['ta'=16,'ha'=16] {'ha'}, dimensions={0} | all-to-all | bytes 819200 | tf_op jit(solution)/shard_map/all_to_all | solution.py:13
  106.1 3.4 stack.47
  109.5 13.4 %all-to-all-start.1 = ((bf16[16,80,2560]{2,1,0:T(8,128)(2,1)}), bf16[16,80,2560]{2,1,0:T(8,128)(2,1)}, u32[]{:S(2)}, u32[]{:S(2)}) async-start(bf16[16,80,2560]{2,1,0:T(8,128)(2,1)} %stack.47), calls=%async_computation.1 | async-start | bytes 13107200 | tf_op jit(solution)/shard_map/all_to_all | solution.py:176
  123.1 192.3 %all-to-all-done.1 = bf16[16,80,2560]{2,1,0:T(8,128)(2,1)} async-done(((bf16[16,80,2560]{2,1,0:T(8,128)(2,1)}), bf16[16,80,2560]{2,1,0:T(8,128)(2,1)}, u32[]{:S(2)}, u32[]{:S(2)}) %all-to-all-start.1) | async-done | bytes 6553632 | tf_op jit(solution)/shard_map/all_to_all | solution.py:176
  315.5 6.0 %convert_multiply_fusion = (f32[128,1280]{1,0:T(8,128)}, bf16[128,1280]{1,0:T(8,128)(2,1)}) fusion(bf16[128,1280]{1,0:T(8,128)(2,1)S(1)} %copy.39, bf16[128,2560]{1,0:T(8,128)(2,1)S(1)} %bitcast.148, bf16[1280,2560]{1,0:T(8,128)(2,1)} %bitcast.21), kind=kOutput, calls=%fused_computation.74 | convolution fusion | flops 839516160 | bytes 8519680 | tf_op jit(solution)/shard_map/dot_general | solution.py:180
  323.1 25.6 %while.29 = (s32[]{:T(128)}, bf16[5,4,128,64]{2,3,1,0:T(8,128)(2,1)}, f32[5,4,576,64]{2,3,1,0:T(8,128)}, f32[5,4,576,64]{2,3,1,0:T(8,128)}, pred[128,576]{0,1:T(...) while((s32[]{:T(128)}, ...), condition=%wide.region_7.8_spmd, body=%wide.region_6.7_spmd.sunk | while | flops 191283200 | bytes 8086649 | solution.py:143
  348.7 3.7 copy.45
  352.4 3.5 copy.46
  355.9 3.3 fusion.48
  360.6 4.1 collective-permute-start.5
  364.7 39.9 %collective-permute-done.4 = f32[6,32,2560]{2,1,0:T(8,128)S(1)} collective-permute-done((f32[6,32,2560]{2,1,0:T(8,128)S(1)}, f32[6,32,2560]{2,1,0:T(8,128)S(1)}, u32[]{:S(2)}, u32[]{:S(2)}) %collective-permute-start.4) | collective-permute-done | bytes 1966112 | tf_op jit(solution)/shard_map/ppermute | solution.py:54
  406.0 5.7 collective-permute-start.6
  415.6 1.9 collective-permute-start.7
  417.5 5.3 collective-permute-done.6
  424.6 108.7 %reduce-scatter.2.cloned.1.call-done = f32[80,2560]{1,0:T(8,128)} async-done(((f32[1280,2560]{1,0:T(8,128)}), f32[80,2560]{1,0:T(8,128)}) %reduce-scatter.2.cloned.1.call-update) | async-done | bytes 819216 | tf_op jit(solution)/shard_map/reduce_scatter | solution.py:204
  533.3 2.4 reshape.354
  535.7 7.8 %all-to-all-start.2 = ((f32[16,5,2560]{2,1,0:T(8,128)}), f32[16,5,2560]{2,1,0:T(8,128)S(1)}, u32[]{:S(2)}, u32[]{:S(2)}) async-start(f32[16,5,2560]{2,1,0:T(8,128)} %reshape.354), calls=%async_computation.3 | async-start | bytes 2621440 | tf_op jit(solution)/shard_map/all_to_all | solution.py:47
  543.5 1.9 fusion.51
  547.6 14.3 %all-to-all-done.2 = f32[16,5,2560]{2,1,0:T(8,128)S(1)} async-done(((f32[16,5,2560]{2,1,0:T(8,128)}), f32[16,5,2560]{2,1,0:T(8,128)S(1)}, u32[]{:S(2)}, u32[]{:S(2)}) %all-to-all-start.2) | async-done | bytes 819232 | tf_op jit(solution)/shard_map/all_to_all | solution.py:47
  (130 shorter events, 61.3 us)
Async XLA Ops:
  7.2 73.4 %copy-start = (bf16[1,4,32,2560]{3,2,1,0:T(8,128)(2,1)S(1)}, bf16[1,4,32,2560]{3,2,1,0:T(8,128)(2,1)}, u32[]{:S(2)}) copy-start(bf16[1,4,32,2560]{3,2,1,0:T(8,128)(2,1)} %param.17) | copy-start | bytes 1966084
  7.2 526.1 %reduce-scatter.2.cloned.1.call-start = ((), (), s32[]{:S(2)}) async-start(), calls=%async_computation.4 | async-start | bytes 13926400 | tf_op jit(solution)/shard_map/reduce_scatter | solution.py:204
  8.3 31.2 %copy-start.9 = (s32[1,4,4,3]{2,1,3,0:T(4,128)S(1)}, s32[1,4,4,3]{2,1,3,0:T(4,128)}, u32[]{:S(2)}) copy-start(s32[1,4,4,3]{2,1,3,0:T(4,128)} %param.19) | copy-start | bytes 580
  8.3 31.5 %copy-start.7 = (bf16[1,4,32,1280]{3,2,1,0:T(8,128)(2,1)S(1)}, bf16[1,4,32,1280]{3,2,1,0:T(8,128)(2,1)}, u32[]{:S(2)}) copy-start(bf16[1,4,32,1280]{3,2,1,0:T(8,128)(2,1)} %param.14) | copy-start | bytes 983044
  9.4 17.8 %collective-permute-start = (bf16[1,4,32,2560]{3,2,1,0:T(8,128)(2,1)S(1)}, bf16[1,4,32,2560]{3,2,1,0:T(8,128)(2,1)S(1)}, u32[]{:S(2)}, u32[]{:S(2)}) collective-permute-start(bf16[1,4,32,2560]{3,2,1,0:T(8,128)(2,1)S(1)} %constant_dynamic-update-slice_fusion), channel_id=1, source_target_pairs={{0,16},{16,32},{32,48},{48,64},{64,80},{80,96},{96,112},{112,128},... | collective-permute-start | bytes 1966088 | tf_op jit(solution)/shard_map/ppermute | solution.py:32
  13.8 17.5 %collective-permute-start.1 = (bf16[1,4,32,2560]{3,2,1,0:T(8,128)(2,1)S(1)}, bf16[1,4,32,2560]{3,2,1,0:T(8,128)(2,1)S(1)}, u32[]{:S(2)}, u32[]{:S(2)}) collective-permute-start(bf16[1,4,32,2560]{3,2,1,0:T(8,128)(2,1)S(1)} %constant_dynamic-update-slice_fusion), channel_id=1, source_target_pairs={{16,0},{32,16},{48,32},{64,48},{80,64},{96,80},{112,96},{128,112},... | collective-permute-start | bytes 1966088 | tf_op jit(solution)/shard_map/ppermute | solution.py:35
  27.1 12.5 %copy-start.2 = (bf16[1,4,32,2560]{3,2,1,0:T(8,128)(2,1)}, bf16[1,4,32,2560]{3,2,1,0:T(8,128)(2,1)S(1)}, u32[]{:S(2)}) copy-start(bf16[1,4,32,2560]{3,2,1,0:T(8,128)(2,1)S(1)} %collective-permute-done) | copy-start | bytes 1966084
  31.3 8.8 %copy-start.3 = (bf16[1,4,32,2560]{3,2,1,0:T(8,128)(2,1)}, bf16[1,4,32,2560]{3,2,1,0:T(8,128)(2,1)S(1)}, u32[]{:S(2)}) copy-start(bf16[1,4,32,2560]{3,2,1,0:T(8,128)(2,1)S(1)} %collective-permute-done.1) | copy-start | bytes 1966084
  32.4 10.7 %collective-permute-start.2 = (bf16[3,1,32,2560]{3,2,1,0:T(8,128)(2,1)}, bf16[3,1,32,2560]{3,2,1,0:T(8,128)(2,1)}, u32[]{:S(2)}, u32[]{:S(2)}) collective-permute-start(bf16[3,1,32,2560]{3,2,1,0:T(8,128)(2,1)} %get-tuple-element.215), channel_id=1, source_target_pairs={{0,1},{1,2},{2,3},{3,4},{4,5},{5,6},{6,7},{7,8},{8,9},{9,10},{10,1... | collective-permute-start | bytes 1474568 | tf_op jit(solution)/shard_map/ppermute | solution.py:32
  37.1 13.0 %collective-permute-start.3 = (bf16[3,1,32,2560]{3,2,1,0:T(8,128)(2,1)}, bf16[3,1,32,2560]{3,2,1,0:T(8,128)(2,1)}, u32[]{:S(2)}, u32[]{:S(2)}) collective-permute-start(bf16[3,1,32,2560]{3,2,1,0:T(8,128)(2,1)} %get-tuple-element.216), channel_id=1, source_target_pairs={{1,0},{2,1},{3,2},{4,3},{5,4},{6,5},{7,6},{8,7},{9,8},{10,9},{11,1... | collective-permute-start | bytes 1474568 | tf_op jit(solution)/shard_map/ppermute | solution.py:35
  80.5 6.6 %copy-start.4 = (bf16[5,4,128,64]{2,3,1,0:T(8,128)(2,1)}, bf16[5,4,128,64]{2,3,1,0:T(8,128)(2,1)S(1)}, u32[]{:S(2)}) copy-start(bf16[5,4,128,64]{2,3,1,0:T(8,128)(2,1)S(1)} %get-tuple-element.126) | copy-start | bytes 983044
  87.1 0.8 copy-start.8
  109.5 13.4 %copy-start.5 = (bf16[5,4,128,64]{2,3,1,0:T(8,128)(2,1)S(1)}, bf16[5,4,128,64]{2,3,1,0:T(8,128)(2,1)}, u32[]{:S(2)}) copy-start(bf16[5,4,128,64]{2,3,1,0:T(8,128)(2,1)} %copy-done.4) | copy-start | bytes 983044
  109.5 206.0 %all-to-all-start.1 = ((bf16[16,80,2560]{2,1,0:T(8,128)(2,1)}), bf16[16,80,2560]{2,1,0:T(8,128)(2,1)}, u32[]{:S(2)}, u32[]{:S(2)}) async-start(bf16[16,80,2560]{2,1,0:T(8,128)(2,1)} %stack.47), calls=%async_computation.1 | async-start | bytes 13107200 | tf_op jit(solution)/shard_map/all_to_all | solution.py:176
  321.5 1.4 copy-start.6
  359.3 45.4 %collective-permute-start.4 = (f32[6,32,2560]{2,1,0:T(8,128)S(1)}, f32[6,32,2560]{2,1,0:T(8,128)S(1)}, u32[]{:S(2)}, u32[]{:S(2)}) collective-permute-start(f32[6,32,2560]{2,1,0:T(8,128)S(1)} %bitcast.159), channel_id=1, source_target_pairs={{16,0},{32,16},{48,32},{64,48},{80,64},{96,80},{112,96},{128,112},... | collective-permute-start | bytes 5898248 | tf_op jit(solution)/shard_map/ppermute | solution.py:54
  360.6 45.0 %collective-permute-start.5 = (f32[6,32,2560]{2,1,0:T(8,128)S(1)}, f32[6,32,2560]{2,1,0:T(8,128)S(1)}, u32[]{:S(2)}, u32[]{:S(2)}) collective-permute-start(f32[6,32,2560]{2,1,0:T(8,128)S(1)} %bitcast.158), channel_id=1, source_target_pairs={{0,16},{16,32},{32,48},{48,64},{64,80},{80,96},{96,112},{112,128},... | collective-permute-start | bytes 5898248 | tf_op jit(solution)/shard_map/ppermute | solution.py:54
  406.0 16.8 %collective-permute-start.6 = (f32[32,2560]{1,0:T(8,128)S(1)}, f32[32,2560]{1,0:T(8,128)}, u32[]{:S(2)}, u32[]{:S(2)}) collective-permute-start(f32[32,2560]{1,0:T(8,128)S(1)} %get-tuple-element.214), channel_id=1, source_target_pairs={{0,1},{1,2},{2,3},{3,4},{4,5},{5,6},{6,7},{7,8},{8,9},{9,10},{10,1... | collective-permute-start | bytes 983048 | tf_op jit(solution)/shard_map/ppermute | solution.py:54
  415.6 127.9 %collective-permute-start.7 = (f32[32,2560]{1,0:T(8,128)S(1)}, f32[32,2560]{1,0:T(8,128)}, u32[]{:S(2)}, u32[]{:S(2)}) collective-permute-start(f32[32,2560]{1,0:T(8,128)S(1)} %get-tuple-element.213), channel_id=1, source_target_pairs={{1,0},{2,1},{3,2},{4,3},{5,4},{6,5},{7,6},{8,7},{9,8},{10,9},{11,1... | collective-permute-start | bytes 983048 | tf_op jit(solution)/shard_map/ppermute | solution.py:54
  535.7 26.3 %all-to-all-start.2 = ((f32[16,5,2560]{2,1,0:T(8,128)}), f32[16,5,2560]{2,1,0:T(8,128)S(1)}, u32[]{:S(2)}, u32[]{:S(2)}) async-start(f32[16,5,2560]{2,1,0:T(8,128)} %reshape.354), calls=%async_computation.3 | async-start | bytes 2621440 | tf_op jit(solution)/shard_map/all_to_all | solution.py:47
  543.5 19.2 %copy-start.1 = (bf16[1,4,32,2560]{3,2,1,0:T(8,128)(2,1)S(1)}, bf16[1,4,32,2560]{3,2,1,0:T(8,128)(2,1)}, u32[]{:S(2)}) copy-start(bf16[1,4,32,2560]{3,2,1,0:T(8,128)(2,1)} %param.17) | copy-start | bytes 1966084
Sparse Core Ops, SparseCore 0:
  87.3 445.9 reduce-scatter.1
